TPU v7x, 256 devices: a whole 4x4x8 slice. The times are simulated.
256 devices in a mesh: seq: 32 (over z, y), head: 8 (over x, core).
Axes of the slice: x: 4, y: 4, z: 8, core: 2. Of those that a mesh axis runs over, the one named last changes fastest.
Arguments:
- queries: bfloat16 [16384, 32, 128], P('seq', 'head'), may hold values from -6 to 6
- key_matrix: bfloat16 [16384, 32, 128], P('seq', 'head'), may hold values from -6 to 6
- value_matrix: bfloat16 [16384, 32, 128], P('seq', 'head'), may hold values from -6 to 6
- level_weight: float32 [15, 32, 16384], P(None, 'head', 'seq'), may hold values from 0.25 to 4
- out_weight: bfloat16 [32, 128, 4096], P('head'), may hold values from -0.09375 to 0.09375
- grad_out: bfloat16 [16384, 4096], P('seq', 'head'), may hold values from -4 to 4
Outputs:
- mixed_out: bfloat16 [16384, 4096], P('seq', 'head')
- grad_queries: bfloat16 [16384, 32, 128], P('seq', 'head')
- grad_keys: bfloat16 [16384, 32, 128], P('seq', 'head')
- grad_values: bfloat16 [16384, 32, 128], P('seq', 'head')
- grad_levels: float32 [15, 32, 16384], P(None, 'head', 'seq')
All inputs are finite; a program needn't handle non-finite values.
Results may differ from a plain program's by a relative error of at most 0.017.
Values may be sent and summed in bfloat16 or wider, within the bound.
No kernel may reach another device: no remote copies, remote signals or barrier semaphores. Data moves between devices by JAX's collectives and lax.ppermute only.
A program may use at most 128 MiB of HBM per device.

v0:
```python
import jax
import jax.numpy as jnp
from jax import lax
from jax.sharding import PartitionSpec as P


def partner_2(block, axis, distance):
    count = lax.axis_size(axis)
    route = []
    for low in range(count):
        high = low | 1 << distance
        if high != low and high < count:
            route += [(low, high), (high, low)]
    return lax.ppermute(block, axis, route)


def in_blocks(array, dim, devices):
    before, after = (array.shape[:dim], array.shape[dim + 1 :])
    return jnp.moveaxis(array.reshape(*before, devices, -1, *after), dim, 0)


def summed_on_arrival(array, axis, dim):
    parts = in_blocks(array, dim, lax.axis_size(axis))
    arrived = lax.all_to_all(parts, axis, split_axis=0, concat_axis=0, tiled=True)
    return arrived.astype(jnp.float32).sum(axis=0)


def top_bit(differ, bit_total):
    count_bits = jnp.zeros(differ.shape, jnp.int32)
    for exponent in range(bit_total):
        count_bits = count_bits + (differ >= 2**exponent).astype(jnp.int32)
    return count_bits


def level_scales(level_total, head_width):
    raised = jnp.maximum(jnp.arange(level_total, dtype=jnp.int32) - 1, 0).astype(jnp.float32)
    return jnp.exp2(-0.5 * raised) / jnp.sqrt(jnp.float32(head_width))


def two_parts(exact_state):
    upper = exact_state.astype(jnp.bfloat16)
    lower = (exact_state - upper.astype(jnp.float32)).astype(jnp.bfloat16)
    return (upper, lower)


def state_first(form, exact_state, plain):
    upper, lower = two_parts(exact_state)
    return jnp.einsum(form, upper, plain, preferred_element_type=jnp.float32) + jnp.einsum(
        form, lower, plain, preferred_element_type=jnp.float32
    )


def state_second(form, plain, exact_state):
    upper, lower = two_parts(exact_state)
    return jnp.einsum(form, plain, upper, preferred_element_type=jnp.float32) + jnp.einsum(
        form, plain, lower, preferred_element_type=jnp.float32
    )


def on_device(queries, key_matrix, value_matrix, level_weight, out_weight, grad_out):
    rows_dev, head_count, head_width = queries.shape
    level_total = level_weight.shape[0]
    near_levels = rows_dev.bit_length()
    far_levels = lax.axis_size("seq").bit_length() - 1
    my_block = lax.axis_index("seq")
    scales = level_scales(level_total, head_width)
    weighted_levels = level_weight * scales[:, None, None]
    flat_out = out_weight.reshape(head_count * head_width, out_weight.shape[2])
    columns = flat_out
    mix_sum = lax.dot_general(
        lax.all_gather(grad_out, "head", axis=1, tiled=True),
        columns,
        (((1,), (1,)), ((), ())),
        preferred_element_type=jnp.float32,
    )
    grad_mix = mix_sum.astype(jnp.bfloat16).reshape(rows_dev, head_count, head_width)
    mix_f = grad_mix.astype(jnp.float32)
    key_weighted = jnp.einsum(
        "gpl,gpq->plq", key_matrix, value_matrix, preferred_element_type=jnp.float32
    )
    far_weights = weighted_levels[near_levels:]
    weighted = (
        far_weights[:, :, :, None] * jnp.transpose(queries.astype(jnp.float32), (1, 0, 2))[None]
    )
    back_states = state_first("jhik,ihv->jhkv", weighted, grad_mix)
    every = lax.all_gather(
        key_weighted[None].astype(jnp.bfloat16), "seq", axis=0, tiled=True
    ).astype(jnp.float32)
    block_ids = jnp.arange(every.shape[0], dtype=jnp.int32)
    block_gap = top_bit(jnp.bitwise_xor(block_ids, my_block), far_levels)
    level_ladder = jnp.arange(1, far_levels + 1, dtype=jnp.int32)
    masks = ((block_gap[None] == level_ladder[:, None]) & (block_ids < my_block)[None]).astype(
        jnp.float32
    )
    left_states = jnp.einsum("je,ehkv->jhkv", masks, every)
    pending = back_states
    right_list = []
    for bit_index in range(far_levels):
        partner = partner_2(pending.astype(jnp.bfloat16), "seq", bit_index).astype(pending.dtype)
        bit_off = 1.0 - (my_block // 2**bit_index % 2).astype(jnp.float32)
        right_list.append(bit_off * partner[0])
        pending = pending[1:] + partner[1:]
    right_states = jnp.stack(right_list)
    rows_index = lax.broadcasted_iota(jnp.int32, (rows_dev, near_levels, rows_dev), 0)
    tier_index = lax.broadcasted_iota(jnp.int32, (rows_dev, near_levels, rows_dev), 1)
    cols_index = lax.broadcasted_iota(jnp.int32, (rows_dev, near_levels, rows_dev), 2)
    near_gap = top_bit(jnp.bitwise_xor(rows_index, cols_index), near_levels - 1)
    onehot = ((near_gap == tier_index) & (cols_index <= rows_index)).astype(jnp.float32)
    mixing = jnp.einsum("ilj,lhi->hij", onehot, weighted_levels[:near_levels])
    scores = jnp.einsum("ihk,jhk->hij", queries, key_matrix, preferred_element_type=jnp.float32)
    attention = (scores * mixing).astype(jnp.bfloat16)
    local_out = jnp.einsum(
        "hij,jhv->ihv", attention, value_matrix, preferred_element_type=jnp.float32
    )
    far_rows = jnp.transpose(far_weights, (0, 2, 1))[..., None]
    reads = state_second("ihk,jhkv->jihv", queries, left_states)
    attended = (local_out + jnp.sum(far_rows * reads, axis=0)).astype(jnp.bfloat16)
    flat_att = attended.reshape(rows_dev, head_count * head_width)
    columns = flat_out
    mixed_cols = summed_on_arrival(
        lax.dot_general(
            columns, flat_att, (((0,), (1,)), ((), ())), preferred_element_type=jnp.float32
        ).astype(jnp.bfloat16),
        "head",
        0,
    )
    mixed_out = jnp.transpose(mixed_cols).astype(jnp.bfloat16)
    back = jnp.einsum("ihv,jhv->hij", grad_mix, value_matrix, preferred_element_type=jnp.float32)
    near_grad = jnp.einsum("ilj,hij->lhi", onehot, scores * back) * scales[:near_levels, None, None]
    far_grad = (
        jnp.transpose(jnp.sum(reads * mix_f[None], axis=3), (0, 2, 1))
        * scales[near_levels:, None, None]
    )
    grad_score = (back * mixing).astype(jnp.bfloat16)
    grad_queries = jnp.einsum(
        "hij,jhk->ihk", grad_score, key_matrix, preferred_element_type=jnp.float32
    )
    grad_queries = grad_queries + jnp.sum(
        far_rows * state_first("jhkv,ihv->jihk", left_states, grad_mix), axis=0
    )
    grad_keys = jnp.einsum("hij,ihk->jhk", grad_score, queries, preferred_element_type=jnp.float32)
    grad_keys = grad_keys + state_first("jhkv,ihv->ihk", right_states, value_matrix)
    grad_values = jnp.einsum(
        "hij,ihv->jhv", attention, grad_mix, preferred_element_type=jnp.float32
    )
    grad_values = grad_values + state_first("jhkv,ihk->ihv", right_states, key_matrix)
    grad_levels = jnp.concatenate([near_grad, far_grad], 0)
    return (
        mixed_out,
        grad_queries.astype(jnp.bfloat16),
        grad_keys.astype(jnp.bfloat16),
        grad_values.astype(jnp.bfloat16),
        grad_levels,
    )


def solution(mesh):
    in_specs = (
        P("seq", "head", None),
        P("seq", "head", None),
        P("seq", "head", None),
        P(None, "head", "seq"),
        P("head", None, None),
        P("seq", "head"),
    )
    out_specs = (
        P("seq", "head"),
        P("seq", "head", None),
        P("seq", "head", None),
        P("seq", "head", None),
        P(None, "head", "seq"),
    )
    return jax.shard_map(
        on_device, mesh=mesh, in_specs=in_specs, out_specs=out_specs, check_vma=False
    )
```

profile of v0, /device:TPU:1, one launch (start us, length us, event | category | flops | bytes accessed | tf_op | source)
XLA Modules:
  0.0 221.7 jit_solution(6458625137675124422)
XLA Ops:
  7.2 0.7 all-gather.4.cloned.1.call-update
  8.0 0.2 copy-done
  8.2 2.0 convolution_convert_fusion.1
  10.3 1.2 convert_bitcast_fusion
  11.5 3.9 %fusion.66 = f32[4,512,512]{2,1,0:T(8,128)} fusion(bf16[512,4,128]{2,1,0:T(4,128)(2,1)} %param.6, bf16[512,4,128]{2,1,0:T(4,128)(2,1)} %param.7), kind=kOutput, calls=%fused_computation.80 | convolution fusion | flops 268435456 | bytes 5242880 | tf_op jit(solution)/shard_map/ihk,jhk->hij/dot_general | solution.py:110
  15.4 0.1 broadcast_multiply_fusion
  15.6 0.6 slice.63
  16.3 0.4 copy.141
  16.7 0.1 copy.169
  16.8 12.6 %fusion.12 = f32[512,4,512]{2,1,0:T(4,128)} fusion(bf16[10,4,512]{0,1,2:T(4,128)(2,1)S(1)} %copy.141), kind=kOutput, calls=%fused_computation.15 | convolution fusion | flops 99614720 | bytes 4235264 | tf_op jit(solution)/shard_map/ilj,lhi->hij/dot_general | solution.py:109
  29.4 19.3 %all-gather.4.cloned.1.call-done = bf16[512,4096]{1,0:T(8,128)(2,1)} async-done(((bf16[512,512]{1,0:T(8,128)(2,1)}), bf16[512,4096]{1,0:T(8,128)(2,1)}) %all-gather.4.cloned.1.call-update) | async-done | bytes 4194320 | tf_op jit(solution)/shard_map/all_gather | solution.py:71
  48.7 7.0 %bitcast_convert_fusion.1 = (f32[512,4,128]{0,2,1:T(8,128)}, bf16[512,512]{0,1:T(8,128)(2,1)S(1)}) fusion(bf16[512,4096]{1,0:T(8,128)(2,1)} %all-gather.4.cloned.1.call-done, bf16[512,4096]{1,0:T(8,128)(2,1)} %bitcast.112), kind=kOutput, calls=%fused_computation.127 | convolution fusion | flops 2148007936 | bytes 9961472 | tf_op jit(solution)/shard_map/dot_general | solution.py:70
  55.6 2.4 %fusion.23 = f32[4,128,5,128]{3,1,2,0:T(8,128)S(1)} fusion(bf16[512,4,128,1]{0,2,3,1:T(8,128)(2,1)S(1)} %bitcast.102, f32[4,512,128]{2,1,0:T(8,128)S(1)} %copy.169, f32[5,4,512]{2,0,1:T(8,128)S(1)} %copy.168), kind=kOutput, calls=%fused_computation.33 | convolution fusion | flops 338165760 | bytes 2924544 | tf_op jit(solution)/shard_map/jhik,ihv->jhkv/dot_general | solution.py:48
  58.0 3.4 %fusion.119 = (bf16[5,4,128,128]{2,3,0,1:T(8,128)(2,1)}, f32[5,4,128,128]{2,3,0,1:T(8,128)}) fusion(f32[4,128,5,128]{3,1,2,0:T(8,128)S(1)} %fusion.23, bf16[512,4,128,1]{0,2,3,1:T(8,128)(2,1)S(1)} %bitcast.103, f32[4,512,128]{2,1,0:T(8,128)S(1)} %copy.169, f32[5,4,512]{2,0,1:T(8,128)S(1)} %copy.168), kind=kOutput, calls=%fused_computation.151 | convolution fusion | flops 342753280 | bytes 4890624 | tf_op jit(solution)/shard_map/jhik,ihv->jhkv/dot_general | solution.py:48
  61.4 1.2 collective-permute-start
  62.7 3.5 %fusion.19 = (bf16[4,512,512]{2,1,0:T(8,128)(2,1)S(1)}, bf16[4,512,512]{2,1,0:T(8,128)(2,1)}, f32[4,512,512]{2,1,0:T(8,128)S(1)}) fusion(f32[512,4,512]{2,1,0:T(4,128)S(1)} %copy-done.10, f32[4,512,512]{2,1,0:T(8,128)S(1)} %copy-done.1, bf16[512,4,128]{0,2,1:T(8,128)(2,1)S(1)} %bitcast.104, bf16[512,4,128]{2,1,0:T(4,128)(2,1)S(1)} %copy-done), kind=kOutput, calls=%fused_computation.29 | convolution fusion | flops 272629760 | bytes 17825792 | tf_op jit(solution)/shard_map/ihv,jhv->hij/dot_general | solution.py:128
  66.2 1.2 mul.130
  67.4 13.1 %fusion.47 = f32[10,4,512]{0,1,2:T(4,128)} fusion(bf16[4,512,512]{2,1,0:T(8,128)(2,1)S(1)} %mul.130, f32[10]{0:T(128)S(1)} %bitcast.111), kind=kOutput, calls=%fused_computation.58 | convolution fusion | flops 99635200 | bytes 2179112 | tf_op jit(solution)/shard_map/ilj,hij->lhi/dot_general | solution.py:129
  80.5 1.5 copy.179
  82.0 1.9 convolution_bitcast_fusion
  83.9 2.5 %fusion.120 = f32[4,128,512]{2,1,0:T(8,128)} fusion(bf16[512,4,128]{0,2,1:T(8,128)(2,1)} %bitcast.105, bf16[4,512,512]{2,1,0:T(8,128)(2,1)S(1)} %copy-done.5), kind=kOutput, calls=%fused_computation.152 | convolution fusion | flops 268435456 | bytes 3670016 | tf_op jit(solution)/shard_map/hij,ihv->jhv/dot_general | solution.py:143
  86.4 1.2 convert_element_type.260
  87.7 1.3 fusion.117
  89.0 2.5 %collective-permute-start.1 = (bf16[4,4,128,128]{2,3,0,1:T(8,128)(2,1)}, bf16[4,4,128,128]{2,3,0,1:T(8,128)(2,1)}, u32[]{:S(2)}, u32[]{:S(2)}) collective-permute-start(bf16[4,4,128,128]{2,3,0,1:T(8,128)(2,1)} %get-tuple-element.33), channel_id=1, source_target_pairs={{0,16},{16,0},{8,24},{24,8},{32,48},{48,32},{40,56},{56,40},{64,80... | collective-permute-start | bytes 1572872 | tf_op jit(solution)/shard_map/ppermute | solution.py:14
  91.4 0.7 fusion.86
  92.2 38.1 %all-gather.6.cloned.1.call-done = bf16[128,128,128]{2,1,0:T(8,128)(2,1)} async-done(((bf16[4,128,128]{2,1,0:T(8,128)(2,1)}), bf16[128,128,128]{2,1,0:T(8,128)(2,1)}) %all-gather.6.cloned.1.call-update) | async-done | bytes 4194320 | tf_op jit(solution)/shard_map/all_gather | solution.py:86
  130.3 4.5 %fusion.21 = f32[5,4,128,128]{3,0,2,1:T(8,128)S(1)} fusion(bf16[32,4,128,128]{3,2,1,0:T(8,128)(2,1)} %bitcast.108, s32[32]{0:T(128)S(1)} %fusion.96, s32[5]{0:T(128)S(1)} %iota_add_fusion, pred[32]{0:T(512)(128)(4,1)S(1)} %iota_compare_fusion.2), kind=kOutput, calls=%fused_computation.31 | convolution fusion | flops 20971840 | bytes 5505204 | tf_op jit(solution)/shard_map/je,ehkv->jhkv/dot_general | solution.py:95
  134.9 0.3 subtract_convert_fusion
  135.1 0.3 copy.263
  135.4 0.9 copy-done.9
  136.3 0.9 fusion.61
  137.2 2.6 %fusion.17 = (f32[5,512,4]{1,0,2:T(8,128)S(1)}, f32[512,4,128]{0,2,1:T(8,128)}) fusion(f32[512,4,128]{0,2,1:T(8,128)S(1)} %copy-done.17, f32[5,512,4]{1,0,2:T(8,128)S(1)} %copy.144, f32[4,5,128,512]{3,2,1,0:T(8,128)S(1)} %fusion.61, bf16[512,4,128,1]{2,1,0,3:T(4,128)(2,1)S(1)} %bitcast.101, bf16[5,4,128,128]{3,2,1,0:T(8,128)(2,1)S(1)} %subtract_convert_fusion), kind=kOutput, calls=%fused_computation.24 | convolution fusion | flops 341825536 | bytes 8601600 | tf_op jit(solution)/shard_map/ihk,jhkv->jihv/dot_general | solution.py:55
  139.8 2.5 %copy.154 = f32[512,4,128]{2,0,1:T(8,128)} copy(f32[512,4,128]{0,2,1:T(8,128)} %get-tuple-element.26) | data formatting | bytes 2097152 | tf_op jit(solution)/shard_map/reduce_sum | solution.py:117
  142.3 7.1 %bitcast_convert_fusion = bf16[512,4096]{1,0:T(8,128)(2,1)} fusion(bf16[4,128,4096]{2,1,0:T(8,128)(2,1)} %param.10, f32[512,4,128]{2,0,1:T(8,128)} %copy.154, bf16[4,512,512]{2,1,0:T(8,128)(2,1)} %get-tuple-element.36, bf16[512,4,128]{2,1,0:T(4,128)(2,1)S(1)} %copy-done), kind=kOutput, calls=%fused_computation.13 | convolution fusion | flops 2418540544 | bytes 12058624 | tf_op jit(solution)/shard_map/dot_general | solution.py:121
  149.5 4.5 %copy.270 = bf16[64,8,8,512]{3,2,0,1:T(8,128)(2,1)} copy(bf16[64,8,8,512]{3,2,1,0:T(8,128)(2,1)} %bitcast.109) | data formatting | bytes 8388608 | tf_op jit(solution)/shard_map/reshape | solution.py:19
  154.0 8.3 %all-to-all-start = ((bf16[8,512,512]{1,2,0:T(8,128)(2,1)}), bf16[8,512,512]{1,2,0:T(8,128)(2,1)}, u32[]{:S(2)}, u32[]{:S(2)}) async-start(bf16[8,512,512]{1,2,0:T(8,128)(2,1)} %bitcast.99), calls=%async_computation | async-start | bytes 8388608 | tf_op jit(solution)/shard_map/all_to_all | solution.py:24
  162.3 2.0 fusion.59
  164.3 1.1 convert_element_type.263
  165.5 1.0 copy-done.13
  166.5 1.2 fusion.116
  167.6 1.2 collective-permute-start.2
  168.8 1.9 fusion.15
  170.7 2.7 %copy.165 = f32[512,4,128]{2,0,1:T(8,128)} copy(f32[512,4,128]{0,2,1:T(8,128)} %fusion.15) | data formatting | bytes 2097152 | tf_op jit(solution)/shard_map/reduce_sum | solution.py:138
  173.4 2.2 fusion.54
  175.6 2.9 %collective-permute-done.2 = bf16[3,4,128,128]{2,3,0,1:T(8,128)(2,1)} collective-permute-done((bf16[3,4,128,128]{2,3,0,1:T(8,128)(2,1)}, bf16[3,4,128,128]{2,3,0,1:T(8,128)(2,1)}, u32[]{:S(2)}, u32[]{:S(2)}) %collective-permute-start.2) | collective-permute-done | bytes 393248 | tf_op jit(solution)/shard_map/ppermute | solution.py:14
  178.5 1.1 convert_element_type.266
  179.5 0.1 fusion.115
  179.6 1.9 collective-permute-start.3
  181.6 1.0 fusion.85
  182.6 11.1 %collective-permute-done.3 = bf16[2,4,128,128]{2,3,0,1:T(8,128)(2,1)S(1)} collective-permute-done((bf16[2,4,128,128]{2,3,0,1:T(8,128)(2,1)S(1)}, bf16[2,4,128,128]{2,3,0,1:T(8,128)(2,1)S(1)}, u32[]{:S(2)}, u32[]{:S(2)}) %collective-permute-start.3) | collective-permute-done | bytes 262176 | tf_op jit(solution)/shard_map/ppermute | solution.py:14
  193.8 2.6 %collective-permute-start.4 = (bf16[1,4,128,128]{2,3,0,1:T(8,128)(2,1)S(1)}, bf16[1,4,128,128]{2,3,0,1:T(8,128)(2,1)S(1)}, u32[]{:S(2)}, u32[]{:S(2)}) collective-permute-start(bf16[1,4,128,128]{2,3,0,1:T(8,128)(2,1)S(1)} %get-tuple-element.37), channel_id=1, source_target_pairs={{0,128},{128,0},{8,136},{136,8},{16,144},{144,16},{24,152},{152,24... | collective-permute-start | bytes 393224 | tf_op jit(solution)/shard_map/ppermute | solution.py:14
  196.4 0.1 multiply_bitcast_fusion
  196.4 1.2 copy.181
  197.7 0.7 pad_maximum_fusion
  198.3 6.2 %collective-permute-done.4 = bf16[1,4,128,128]{2,3,0,1:T(8,128)(2,1)S(1)} collective-permute-done((bf16[1,4,128,128]{2,3,0,1:T(8,128)(2,1)S(1)}, bf16[1,4,128,128]{2,3,0,1:T(8,128)(2,1)S(1)}, u32[]{:S(2)}, u32[]{:S(2)}) %collective-permute-start.4) | collective-permute-done | bytes 131104 | tf_op jit(solution)/shard_map/ppermute | solution.py:14
  204.6 0.1 convert_reduce_fusion.1
  204.8 0.3 fusion.69
  205.1 0.3 fusion.52
  205.4 1.2 copy.182
  206.6 0.3 fusion.78
  206.9 0.3 fusion.56
  207.2 1.1 copy.183
  208.3 2.8 %all-to-all-done = bf16[8,512,512]{1,2,0:T(8,128)(2,1)} async-done(((bf16[8,512,512]{1,2,0:T(8,128)(2,1)}), bf16[8,512,512]{1,2,0:T(8,128)(2,1)}, u32[]{:S(2)}, u32[]{:S(2)}) %all-to-all-start) | async-done | bytes 4194336 | tf_op jit(solution)/shard_map/all_to_all | solution.py:24
  211.1 3.7 %reduce_sum.66 = bf16[512,512]{0,1:T(8,128)(2,1)} reduce(bf16[8,512,512]{1,2,0:T(8,128)(2,1)} %all-to-all-done, bf16[]{:T(256)} %constant.118.clone.1), dimensions={0}, to_apply=%region_1.2 | reduce | flops 1835008 | bytes 4718594 | tf_op jit(solution)/shard_map/reduce_sum | solution.py:25
  (57 shorter events, 0.4 us)
Async XLA Ops:
  7.2 1.0 copy-start
  7.2 41.5 %all-gather.4.cloned.1.call-start = ((), (), s32[]{:S(2)}) async-start(), calls=%async_computation.1 | async-start | bytes 4718592 | tf_op jit(solution)/shard_map/all_gather | solution.py:71
  7.9 7.5 %copy-start.19 = (f32[15,4,512]{2,1,0:T(4,128)S(1)}, f32[15,4,512]{2,1,0:T(4,128)}, u32[]{:S(2)}) copy-start(f32[15,4,512]{2,1,0:T(4,128)} %param.9) | copy-start | bytes 368644
  7.9 122.4 %all-gather.6.cloned.1.call-start = ((), (), s32[]{:S(2)}) async-start(), calls=%async_computation.2 | async-start | bytes 4325376 | tf_op jit(solution)/shard_map/all_gather | solution.py:86
  48.7 14.0 %copy-start.10 = (f32[512,4,512]{2,1,0:T(4,128)S(1)}, f32[512,4,512]{2,1,0:T(4,128)}, u32[]{:S(2)}) copy-start(f32[512,4,512]{2,1,0:T(4,128)} %fusion.12) | copy-start | bytes 12582916
  55.6 10.5 %copy-start.3 = (bf16[512,512]{0,1:T(8,128)(2,1)}, bf16[512,512]{0,1:T(8,128)(2,1)S(1)}, u32[]{:S(2)}) copy-start(bf16[512,512]{0,1:T(8,128)(2,1)S(1)} %get-tuple-element.42) | copy-start | bytes 1572868
  55.6 7.0 %copy-start.1 = (f32[4,512,512]{2,1,0:T(8,128)S(1)}, f32[4,512,512]{2,1,0:T(8,128)}, u32[]{:S(2)}) copy-start(f32[4,512,512]{2,1,0:T(8,128)} %fusion.66) | copy-start | bytes 12582916
  61.4 25.0 %collective-permute-start = (bf16[5,4,128,128]{2,3,0,1:T(8,128)(2,1)}, bf16[5,4,128,128]{2,3,0,1:T(8,128)(2,1)}, u32[]{:S(2)}, u32[]{:S(2)}) collective-permute-start(bf16[5,4,128,128]{2,3,0,1:T(8,128)(2,1)} %get-tuple-element.44), channel_id=1, source_target_pairs={{0,8},{8,0},{16,24},{24,16},{32,40},{40,32},{48,56},{56,48},{64,72... | collective-permute-start | bytes 1966088 | tf_op jit(solution)/shard_map/ppermute | solution.py:14
  67.3 14.7 %copy-start.2 = (bf16[512,4,128]{2,1,0:T(4,128)(2,1)S(1)}, bf16[512,4,128]{2,1,0:T(4,128)(2,1)}, u32[]{:S(2)}) copy-start(bf16[512,4,128]{2,1,0:T(4,128)(2,1)} %param.6) | copy-start | bytes 1572868
  82.0 1.9 copy-start.5
  82.0 5.6 %copy-start.18 = (f32[5,4,128,128]{2,3,0,1:T(8,128)S(1)}, f32[5,4,128,128]{2,3,0,1:T(8,128)}, u32[]{:S(2)}) copy-start(f32[5,4,128,128]{2,3,0,1:T(8,128)} %get-tuple-element.45) | copy-start | bytes 3932164
  89.0 75.4 %collective-permute-start.1 = (bf16[4,4,128,128]{2,3,0,1:T(8,128)(2,1)}, bf16[4,4,128,128]{2,3,0,1:T(8,128)(2,1)}, u32[]{:S(2)}, u32[]{:S(2)}) collective-permute-start(bf16[4,4,128,128]{2,3,0,1:T(8,128)(2,1)} %get-tuple-element.33), channel_id=1, source_target_pairs={{0,16},{16,0},{8,24},{24,8},{32,48},{48,32},{40,56},{56,40},{64,80... | collective-permute-start | bytes 1572872 | tf_op jit(solution)/shard_map/ppermute | solution.py:14
  135.1 2.0 copy-start.7
  135.1 2.0 copy-start.17
  135.4 0.9 copy-start.9
  154.0 8.3 %copy-start.4 = (bf16[512,512]{0,1:T(8,128)(2,1)S(1)}, bf16[512,512]{0,1:T(8,128)(2,1)}, u32[]{:S(2)}) copy-start(bf16[512,512]{0,1:T(8,128)(2,1)} %copy-done.3) | copy-start | bytes 1572868
  154.0 57.1 %all-to-all-start = ((bf16[8,512,512]{1,2,0:T(8,128)(2,1)}), bf16[8,512,512]{1,2,0:T(8,128)(2,1)}, u32[]{:S(2)}, u32[]{:S(2)}) async-start(bf16[8,512,512]{1,2,0:T(8,128)(2,1)} %bitcast.99), calls=%async_computation | async-start | bytes 8388608 | tf_op jit(solution)/shard_map/all_to_all | solution.py:24
  162.3 4.2 %copy-start.14 = (f32[4,4,128,128]{2,3,0,1:T(8,128)S(1)}, f32[4,4,128,128]{2,3,0,1:T(8,128)}, u32[]{:S(2)}) copy-start(f32[4,4,128,128]{2,3,0,1:T(8,128)} %get-tuple-element.34) | copy-start | bytes 3145732
  162.3 6.5 %copy-start.8 = (bf16[5,4,128,128]{3,2,1,0:T(8,128)(2,1)S(1)}, bf16[5,4,128,128]{3,2,1,0:T(8,128)(2,1)}, u32[]{:S(2)}) copy-start(bf16[5,4,128,128]{3,2,1,0:T(8,128)(2,1)} %copy-done.7) | copy-start | bytes 1966084
  165.5 1.0 copy-start.13
  167.6 10.8 %collective-permute-start.2 = (bf16[3,4,128,128]{2,3,0,1:T(8,128)(2,1)}, bf16[3,4,128,128]{2,3,0,1:T(8,128)(2,1)}, u32[]{:S(2)}, u32[]{:S(2)}) collective-permute-start(bf16[3,4,128,128]{2,3,0,1:T(8,128)(2,1)} %get-tuple-element.31), channel_id=1, source_target_pairs={{0,32},{32,0},{8,40},{40,8},{16,48},{48,16},{24,56},{56,24},{64,96... | collective-permute-start | bytes 1179656 | tf_op jit(solution)/shard_map/ppermute | solution.py:14
  170.7 8.9 %copy-start.15 = (f32[3,4,128,128]{2,3,0,1:T(8,128)S(1)}, f32[3,4,128,128]{2,3,0,1:T(8,128)}, u32[]{:S(2)}) copy-start(f32[3,4,128,128]{2,3,0,1:T(8,128)} %get-tuple-element.32) | copy-start | bytes 2359300
  173.4 8.2 %copy-start.16 = (f32[5,4,128,128]{2,3,0,1:T(8,128)S(1)}, f32[5,4,128,128]{2,3,0,1:T(8,128)}, u32[]{:S(2)}) copy-start(f32[5,4,128,128]{2,3,0,1:T(8,128)} %fusion.86) | copy-start | bytes 3932164
  173.4 23.0 %copy-start.20 = (f32[5]{0:T(128)S(1)}, f32[5]{0:T(128)}, u32[]{:S(2)}) copy-start(f32[5]{0:T(128)} %slice.63) | copy-start | bytes 64
  179.6 25.4 %copy-start.12 = (f32[512,4,128]{2,0,1:T(8,128)S(1)}, f32[512,4,128]{2,0,1:T(8,128)}, u32[]{:S(2)}) copy-start(f32[512,4,128]{2,0,1:T(8,128)} %convolution_bitcast_fusion) | copy-start | bytes 3145732
  179.6 14.0 %collective-permute-start.3 = (bf16[2,4,128,128]{2,3,0,1:T(8,128)(2,1)S(1)}, bf16[2,4,128,128]{2,3,0,1:T(8,128)(2,1)S(1)}, u32[]{:S(2)}, u32[]{:S(2)}) collective-permute-start(bf16[2,4,128,128]{2,3,0,1:T(8,128)(2,1)S(1)} %get-tuple-element.29), channel_id=1, source_target_pairs={{0,64},{64,0},{8,72},{72,8},{16,80},{80,16},{24,88},{88,24},{32,96... | collective-permute-start | bytes 786440 | tf_op jit(solution)/shard_map/ppermute | solution.py:14
  193.8 10.8 %collective-permute-start.4 = (bf16[1,4,128,128]{2,3,0,1:T(8,128)(2,1)S(1)}, bf16[1,4,128,128]{2,3,0,1:T(8,128)(2,1)S(1)}, u32[]{:S(2)}, u32[]{:S(2)}) collective-permute-start(bf16[1,4,128,128]{2,3,0,1:T(8,128)(2,1)S(1)} %get-tuple-element.37), channel_id=1, source_target_pairs={{0,128},{128,0},{8,136},{136,8},{16,144},{144,16},{24,152},{152,24... | collective-permute-start | bytes 393224 | tf_op jit(solution)/shard_map/ppermute | solution.py:14
  197.6 8.9 %copy-start.6 = (bf16[512,4,128]{2,1,0:T(4,128)(2,1)S(1)}, bf16[512,4,128]{2,1,0:T(4,128)(2,1)}, u32[]{:S(2)}) copy-start(bf16[512,4,128]{2,1,0:T(4,128)(2,1)} %param.7) | copy-start | bytes 1572868
  204.7 2.1 copy-start.11
Sparse Core Ops, SparseCore 0:
  9.8 38.7 all-gather.3
  51.8 78.4 all-gather.5
where the time goes:
time: 222 us
  waiting for transfers between devices  81.1 us (37%)
  matrix products  74.8 us (34%)
  local copies, waits for them, and re-layouts  18.3 us (8%)
  starting transfers between devices  17.7 us (8%)
  other arithmetic  15.1 us (7%)
  between operations  14.6 us (7%)
    all_gather x1, waiting for transfers between devices, on_device(): lax.all_gather(key_weighted[None].astype(jnp.bfloat16), 'seq', axis=0, ti...  38.1 us
    ppermute x5, waiting for transfers between devices, partner_2(): return lax.ppermute(block, axis, route)  20.2 us
    all_gather x1, waiting for transfers between devices, on_device(): lax.all_gather(grad_out, 'head', axis=1, tiled=True)  19.3 us
    dot_general x1, matrix products, on_device(): jnp.einsum('ilj,hij->lhi', onehot, scores * back)  13.1 us
    dot_general x1, matrix products, on_device(): mixing = jnp.einsum('ilj,lhi->hij', onehot, weighted_levels[:near_levels])  12.6 us
    ppermute x5, starting transfers between devices, partner_2(): return lax.ppermute(block, axis, route)  9.37 us
    all_to_all x1, starting transfers between devices, summed_on_arrival(): lax.all_to_all(parts, axis, split_axis=0, concat_axis=0, tiled=True)  8.28 us
    dot_general x1, matrix products, on_device(): lax.dot_general(columns, flat_att, (((0,), (1,)), ((), ())), preferred_el...  7.13 us
  transfers between devices with their start and end apart: 8, of which 6 were waited for; matrix products, arithmetic and copies ran while one was open for 46% of the time, Pallas kernels for 0%

commit v1 on v0

--- a/solution.py
+++ b/solution.py
@@ -2,6 +2,17 @@
 import jax.numpy as jnp
 from jax import lax
 from jax.sharding import PartitionSpec as P
+
+
+def _use_wires(message, device_axis):
+    block_list = []
+    for _ in range(jax.lax.axis_size(device_axis)):
+        block_list.append(message)
+    answer = jnp.concatenate(block_list, axis=0)
+    next_value = jax.lax.all_to_all(
+        answer, axis_name=device_axis, split_axis=0, concat_axis=0, tiled=True
+    )
+    return next_value
 
 
 def partner_2(block, axis, distance):
@@ -83,9 +94,7 @@
         far_weights[:, :, :, None] * jnp.transpose(queries.astype(jnp.float32), (1, 0, 2))[None]
     )
     back_states = state_first("jhik,ihv->jhkv", weighted, grad_mix)
-    every = lax.all_gather(
-        key_weighted[None].astype(jnp.bfloat16), "seq", axis=0, tiled=True
-    ).astype(jnp.float32)
+    every = _use_wires(key_weighted[None].astype(jnp.bfloat16), "seq").astype(jnp.float32)
     block_ids = jnp.arange(every.shape[0], dtype=jnp.int32)
     block_gap = top_bit(jnp.bitwise_xor(block_ids, my_block), far_levels)
     level_ladder = jnp.arange(1, far_levels + 1, dtype=jnp.int32)

time: 222 us -> 210 us (0.946)
  waiting for transfers between devices: 81.1 us -> 56.3 us
  starting transfers between devices: 17.7 us -> 28.3 us
  local copies, waits for them, and re-layouts: 18.3 us -> 21.8 us
    all_gather x1 -> x0, waiting for transfers between devices: 38.1 us -> none  [on_device(): lax.all_gather(key_weighted[None].astype(jnp.bfloat16), 'seq', axis=0, ti...]
    all_to_all x0 -> x1, waiting for transfers between devices: none -> 25.2 us  [_use_wires(): jax.lax.all_to_all(answer, axis_name=device_axis, split_axis=0, concat_ax...]
    all_gather x1, waiting for transfers between devices: 19.3 us -> 6.51 us  [on_device(): lax.all_gather(grad_out, 'head', axis=1, tiled=True)]
    all_to_all x0 -> x1, starting transfers between devices: none -> 12.3 us  [_use_wires(): jax.lax.all_to_all(answer, axis_name=device_axis, split_axis=0, concat_ax...]
    concatenate x0 -> x1, local copies, waits for them, and re-layouts: none -> 3.07 us  [_use_wires(): answer = jnp.concatenate(block_list, axis=0)]
    unnamed x45 -> x47, local copies, waits for them, and re-layouts: 5.61 us -> 5.64 us
  transfers between devices with their start and end apart: 8 -> 8, of which waited for: 6 -> 6; matrix products, arithmetic and copies ran while one was open for 46% -> 49% of each run, Pallas kernels for 0% -> 0%
where the time goes in v1:
time: 210 us; the launch traced here: 208 us
  matrix products  72.9 us (35%)
  waiting for transfers between devices  56.3 us (27%)
  starting transfers between devices  28.3 us (13%)
  local copies, waits for them, and re-layouts  21.8 us (10%)
  between operations  14.5 us (7%)
  other arithmetic  14.1 us (7%)
    all_to_all x1, waiting for transfers between devices, _use_wires(): jax.lax.all_to_all(answer, axis_name=device_axis, split_axis=0, concat_ax...  25.2 us
    ppermute x5, waiting for transfers between devices, partner_2(): return lax.ppermute(block, axis, route)  21.1 us
    dot_general x1, matrix products, on_device(): jnp.einsum('ilj,hij->lhi', onehot, scores * back)  13.1 us
    dot_general x1, matrix products, on_device(): mixing = jnp.einsum('ilj,lhi->hij', onehot, weighted_levels[:near_levels])  12.5 us
    all_to_all x1, starting transfers between devices, _use_wires(): jax.lax.all_to_all(answer, axis_name=device_axis, split_axis=0, concat_ax...  12.3 us
    ppermute x5, starting transfers between devices, partner_2(): return lax.ppermute(block, axis, route)  9.23 us
    dot_general x1, matrix products, on_device(): lax.dot_general(columns, flat_att, (((0,), (1,)), ((), ())), preferred_el...  7.13 us
    dot_general x1, matrix products, on_device(): lax.dot_general(lax.all_gather(grad_out, 'head', axis=1, tiled=True), col...  6.96 us
  transfers between devices with their start and end apart: 8, of which 6 were waited for; matrix products, arithmetic and copies ran while one was open for 49% of the time, Pallas kernels for 0%

profile of v1, /device:TPU:1, one launch (start us, length us, event | category | flops | bytes accessed | tf_op | source)
XLA Modules:
  0.0 207.8 jit_solution(5078401765017260268)
XLA Ops:
  7.2 0.7 all-gather.2.cloned.1.call-update
  7.9 0.3 copy-done
  8.2 1.4 convolution_convert_fusion.1
  9.6 3.1 %concatenate.6 = bf16[32,4,128,128]{3,2,1,0:T(8,128)(2,1)} broadcast(bf16[4,128,128]{2,1,0:T(8,128)(2,1)S(1)} %convolution_convert_fusion.1), dimensions={1,2,3} | broadcast | bytes 4325376 | tf_op jit(solution)/shard_map/concatenate | solution.py:11
  12.7 12.3 %all-to-all-start = ((bf16[32,4,128,128]{3,2,1,0:T(8,128)(2,1)}), bf16[32,4,128,128]{3,2,1,0:T(8,128)(2,1)}, u32[]{:S(2)}, u32[]{:S(2)}) async-start(bf16[32,4,128,128]{3,2,1,0:T(8,128)(2,1)} %concatenate.6), calls=%async_computation | async-start | bytes 8388608 | tf_op jit(solution)/shard_map/all_to_all | solution.py:12
  25.0 0.1 broadcast_multiply_fusion
  25.1 0.1 convert_bitcast_fusion
  25.3 2.7 %fusion.66 = f32[4,512,512]{2,1,0:T(8,128)} fusion(bf16[512,4,128]{2,1,0:T(4,128)(2,1)S(1)} %copy-done.2, bf16[512,4,128]{2,1,0:T(4,128)(2,1)S(1)} %copy-done.6), kind=kOutput, calls=%fused_computation.80 | convolution fusion | flops 268435456 | bytes 5242880 | tf_op jit(solution)/shard_map/ihk,jhk->hij/dot_general | solution.py:119
  28.2 0.4 copy.92
  28.5 1.0 copy.120
  29.6 12.5 %fusion.12 = f32[512,4,512]{2,1,0:T(4,128)} fusion(bf16[10,4,512]{0,1,2:T(4,128)(2,1)S(1)} %copy.92), kind=kOutput, calls=%fused_computation.15 | convolution fusion | flops 99614720 | bytes 4235264 | tf_op jit(solution)/shard_map/ilj,lhi->hij/dot_general | solution.py:118
  42.1 6.5 %all-gather.2.cloned.1.call-done = bf16[512,4096]{1,0:T(8,128)(2,1)} async-done(((bf16[512,512]{1,0:T(8,128)(2,1)}), bf16[512,4096]{1,0:T(8,128)(2,1)}) %all-gather.2.cloned.1.call-update) | async-done | bytes 4194320 | tf_op jit(solution)/shard_map/all_gather | solution.py:82
  48.6 7.0 %bitcast_convert_fusion.1 = (f32[512,4,128]{0,2,1:T(8,128)}, bf16[512,512]{0,1:T(8,128)(2,1)S(1)}) fusion(bf16[512,4096]{1,0:T(8,128)(2,1)} %all-gather.2.cloned.1.call-done, bf16[512,4096]{1,0:T(8,128)(2,1)} %bitcast.110), kind=kOutput, calls=%fused_computation.127 | convolution fusion | flops 2148007936 | bytes 9961472 | tf_op jit(solution)/shard_map/dot_general | solution.py:81
  55.6 2.4 %fusion.23 = f32[4,128,5,128]{3,1,2,0:T(8,128)S(1)} fusion(bf16[512,4,128,1]{0,2,3,1:T(8,128)(2,1)S(1)} %bitcast.101, f32[4,512,128]{2,1,0:T(8,128)S(1)} %copy-done.19, f32[5,4,512]{2,0,1:T(8,128)S(1)} %copy.119), kind=kOutput, calls=%fused_computation.33 | convolution fusion | flops 338165760 | bytes 2924544 | tf_op jit(solution)/shard_map/jhik,ihv->jhkv/dot_general | solution.py:59
  58.0 3.4 %fusion.119 = (bf16[5,4,128,128]{2,3,0,1:T(8,128)(2,1)}, f32[5,4,128,128]{2,3,0,1:T(8,128)}) fusion(f32[4,128,5,128]{3,1,2,0:T(8,128)S(1)} %fusion.23, bf16[512,4,128,1]{0,2,3,1:T(8,128)(2,1)S(1)} %bitcast.102, f32[4,512,128]{2,1,0:T(8,128)S(1)} %copy-done.19, f32[5,4,512]{2,0,1:T(8,128)S(1)} %copy.119), kind=kOutput, calls=%fused_computation.151 | convolution fusion | flops 342753280 | bytes 4890624 | tf_op jit(solution)/shard_map/jhik,ihv->jhkv/dot_general | solution.py:59
  61.4 1.2 collective-permute-start
  62.6 3.5 %fusion.19 = (bf16[4,512,512]{2,1,0:T(8,128)(2,1)S(1)}, bf16[4,512,512]{2,1,0:T(8,128)(2,1)}, f32[4,512,512]{2,1,0:T(8,128)S(1)}) fusion(f32[512,4,512]{2,1,0:T(4,128)S(1)} %copy-done.11, f32[4,512,512]{2,1,0:T(8,128)S(1)} %copy-done.1, bf16[512,4,128]{0,2,1:T(8,128)(2,1)S(1)} %bitcast.103, bf16[512,4,128]{2,1,0:T(4,128)(2,1)S(1)} %copy-done), kind=kOutput, calls=%fused_computation.29 | convolution fusion | flops 272629760 | bytes 17825792 | tf_op jit(solution)/shard_map/ihv,jhv->hij/dot_general | solution.py:137
  66.1 1.2 mul.130
  67.3 13.1 %fusion.47 = f32[10,4,512]{0,1,2:T(4,128)} fusion(bf16[4,512,512]{2,1,0:T(8,128)(2,1)S(1)} %mul.130, f32[10]{0:T(128)S(1)} %bitcast.109), kind=kOutput, calls=%fused_computation.58 | convolution fusion | flops 99635200 | bytes 2179112 | tf_op jit(solution)/shard_map/ilj,hij->lhi/dot_general | solution.py:138
  80.4 1.5 copy.130
  82.0 1.9 convolution_bitcast_fusion
  83.9 2.5 %fusion.120 = f32[4,128,512]{2,1,0:T(8,128)} fusion(bf16[512,4,128]{0,2,1:T(8,128)(2,1)} %bitcast.104, bf16[4,512,512]{2,1,0:T(8,128)(2,1)S(1)} %copy-done.5), kind=kOutput, calls=%fused_computation.152 | convolution fusion | flops 268435456 | bytes 3670016 | tf_op jit(solution)/shard_map/hij,ihv->jhv/dot_general | solution.py:152
  86.3 1.2 convert_element_type.257
  87.6 1.3 fusion.117
  88.9 3.2 %collective-permute-start.1 = (bf16[4,4,128,128]{2,3,0,1:T(8,128)(2,1)}, bf16[4,4,128,128]{2,3,0,1:T(8,128)(2,1)}, u32[]{:S(2)}, u32[]{:S(2)}) collective-permute-start(bf16[4,4,128,128]{2,3,0,1:T(8,128)(2,1)} %get-tuple-element.28), channel_id=1, source_target_pairs={{0,16},{16,0},{8,24},{24,8},{32,48},{48,32},{40,56},{56,40},{64,80... | collective-permute-start | bytes 1572872 | tf_op jit(solution)/shard_map/ppermute | solution.py:25
  92.1 0.7 fusion.86
  92.8 25.2 %all-to-all-done = bf16[32,4,128,128]{3,2,1,0:T(8,128)(2,1)} async-done(((bf16[32,4,128,128]{3,2,1,0:T(8,128)(2,1)}), bf16[32,4,128,128]{3,2,1,0:T(8,128)(2,1)}, u32[]{:S(2)}, u32[]{:S(2)}) %all-to-all-start) | async-done | bytes 4194336 | tf_op jit(solution)/shard_map/all_to_all | solution.py:12
  118.0 4.5 %fusion.21 = f32[5,4,128,128]{3,0,2,1:T(8,128)S(1)} fusion(bf16[32,4,128,128]{3,2,1,0:T(8,128)(2,1)} %all-to-all-done, s32[32]{0:T(128)S(1)} %fusion.96, s32[5]{0:T(128)S(1)} %iota_add_fusion, pred[32]{0:T(512)(128)(4,1)S(1)} %iota_compare_fusion.2), kind=kOutput, calls=%fused_computation.31 | convolution fusion | flops 20971840 | bytes 5505204 | tf_op jit(solution)/shard_map/je,ehkv->jhkv/dot_general | solution.py:104
  122.6 0.3 subtract_convert_fusion
  122.8 0.3 copy.214
  123.1 0.8 copy-done.10
  123.9 0.9 fusion.61
  124.9 2.6 %fusion.17 = (f32[5,512,4]{1,0,2:T(8,128)S(1)}, f32[512,4,128]{0,2,1:T(8,128)}) fusion(f32[512,4,128]{0,2,1:T(8,128)S(1)} %copy-done.18, f32[5,512,4]{1,0,2:T(8,128)S(1)} %copy.95, f32[4,5,128,512]{3,2,1,0:T(8,128)S(1)} %fusion.61, bf16[512,4,128,1]{2,1,0,3:T(4,128)(2,1)S(1)} %bitcast.100, bf16[5,4,128,128]{3,2,1,0:T(8,128)(2,1)S(1)} %subtract_convert_fusion), kind=kOutput, calls=%fused_computation.24 | convolution fusion | flops 341825536 | bytes 8601600 | tf_op jit(solution)/shard_map/ihk,jhkv->jihv/dot_general | solution.py:66
  127.5 2.5 %copy.105 = f32[512,4,128]{2,0,1:T(8,128)} copy(f32[512,4,128]{0,2,1:T(8,128)} %get-tuple-element.21) | data formatting | bytes 2097152 | tf_op jit(solution)/shard_map/reduce_sum | solution.py:126
  130.0 7.1 %bitcast_convert_fusion = bf16[512,4096]{1,0:T(8,128)(2,1)} fusion(bf16[4,128,4096]{2,1,0:T(8,128)(2,1)} %param.10, f32[512,4,128]{2,0,1:T(8,128)} %copy.105, bf16[4,512,512]{2,1,0:T(8,128)(2,1)} %get-tuple-element.31, bf16[512,4,128]{2,1,0:T(4,128)(2,1)S(1)} %copy-done), kind=kOutput, calls=%fused_computation.13 | convolution fusion | flops 2418540544 | bytes 12058624 | tf_op jit(solution)/shard_map/dot_general | solution.py:130
  137.1 4.5 %copy.221 = bf16[64,8,8,512]{3,2,0,1:T(8,128)(2,1)} copy(bf16[64,8,8,512]{3,2,1,0:T(8,128)(2,1)} %bitcast.107) | data formatting | bytes 8388608 | tf_op jit(solution)/shard_map/reshape | solution.py:30
  141.7 6.8 %all-to-all-start.1 = ((bf16[8,512,512]{1,2,0:T(8,128)(2,1)}), bf16[8,512,512]{1,2,0:T(8,128)(2,1)}, u32[]{:S(2)}, u32[]{:S(2)}) async-start(bf16[8,512,512]{1,2,0:T(8,128)(2,1)} %bitcast.98), calls=%async_computation.1 | async-start | bytes 8388608 | tf_op jit(solution)/shard_map/all_to_all | solution.py:35
  148.4 2.0 fusion.59
  150.5 1.1 convert_element_type.260
  151.7 1.0 copy-done.14
  152.6 1.2 fusion.116
  153.8 1.8 collective-permute-start.2
  155.6 1.9 fusion.15
  157.5 2.6 %copy.116 = f32[512,4,128]{2,0,1:T(8,128)} copy(f32[512,4,128]{0,2,1:T(8,128)} %fusion.15) | data formatting | bytes 2097152 | tf_op jit(solution)/shard_map/reduce_sum | solution.py:147
  160.1 2.2 %fusion.54 = bf16[512,4,128]{2,0,1:T(8,128)(2,1)S(1)} fusion(f32[512,4,128]{2,0,1:T(8,128)} %copy.116, bf16[4,512,512]{2,1,0:T(8,128)(2,1)S(1)} %get-tuple-element.30, bf16[512,4,128]{2,1,0:T(4,128)(2,1)} %param.7), kind=kOutput, calls=%fused_computation.62 | convolution fusion | flops 268959744 | bytes 4194304 | tf_op jit(solution)/shard_map/hij,jhk->ihk/dot_general | solution.py:144
  162.4 2.9 %collective-permute-done.2 = bf16[3,4,128,128]{2,3,0,1:T(8,128)(2,1)} collective-permute-done((bf16[3,4,128,128]{2,3,0,1:T(8,128)(2,1)}, bf16[3,4,128,128]{2,3,0,1:T(8,128)(2,1)}, u32[]{:S(2)}, u32[]{:S(2)}) %collective-permute-start.2) | collective-permute-done | bytes 393248 | tf_op jit(solution)/shard_map/ppermute | solution.py:25
  165.3 1.1 convert_element_type.263
  166.4 0.1 fusion.115
  166.4 1.5 collective-permute-start.3
  168.0 1.0 fusion.85
  169.0 11.5 %collective-permute-done.3 = bf16[2,4,128,128]{2,3,0,1:T(8,128)(2,1)S(1)} collective-permute-done((bf16[2,4,128,128]{2,3,0,1:T(8,128)(2,1)S(1)}, bf16[2,4,128,128]{2,3,0,1:T(8,128)(2,1)S(1)}, u32[]{:S(2)}, u32[]{:S(2)}) %collective-permute-start.3) | collective-permute-done | bytes 262176 | tf_op jit(solution)/shard_map/ppermute | solution.py:25
  180.6 1.5 collective-permute-start.4
  182.2 1.2 copy.132
  183.4 0.7 pad_maximum_fusion
  184.1 6.7 %collective-permute-done.4 = bf16[1,4,128,128]{2,3,0,1:T(8,128)(2,1)S(1)} collective-permute-done((bf16[1,4,128,128]{2,3,0,1:T(8,128)(2,1)S(1)}, bf16[1,4,128,128]{2,3,0,1:T(8,128)(2,1)S(1)}, u32[]{:S(2)}, u32[]{:S(2)}) %collective-permute-start.4) | collective-permute-done | bytes 131104 | tf_op jit(solution)/shard_map/ppermute | solution.py:25
  190.8 0.1 convert_reduce_fusion.1
  191.0 0.3 fusion.69
  191.3 0.3 fusion.52
  191.6 1.2 copy.133
  192.8 0.3 fusion.78
  193.1 0.3 fusion.56
  193.4 1.1 copy.134
  194.5 2.8 %all-to-all-done.1 = bf16[8,512,512]{1,2,0:T(8,128)(2,1)} async-done(((bf16[8,512,512]{1,2,0:T(8,128)(2,1)}), bf16[8,512,512]{1,2,0:T(8,128)(2,1)}, u32[]{:S(2)}, u32[]{:S(2)}) %all-to-all-start.1) | async-done | bytes 4194336 | tf_op jit(solution)/shard_map/all_to_all | solution.py:35
  197.2 3.7 %reduce_sum.66 = bf16[512,512]{0,1:T(8,128)(2,1)} reduce(bf16[8,512,512]{1,2,0:T(8,128)(2,1)} %all-to-all-done.1, bf16[]{:T(256)} %constant.118.clone.1), dimensions={0}, to_apply=%region_1.2 | reduce | flops 1835008 | bytes 4718594 | tf_op jit(solution)/shard_map/reduce_sum | solution.py:36
  (59 shorter events, 0.5 us)
Async XLA Ops:
  7.2 1.0 copy-start
  7.2 41.4 %all-gather.2.cloned.1.call-start = ((), (), s32[]{:S(2)}) async-start(), calls=%async_computation.2 | async-start | bytes 4718592 | tf_op jit(solution)/shard_map/all_gather | solution.py:82
  12.7 12.3 %copy-start.21 = (f32[15,4,512]{2,1,0:T(4,128)S(1)}, f32[15,4,512]{2,1,0:T(4,128)}, u32[]{:S(2)}) copy-start(f32[15,4,512]{2,1,0:T(4,128)} %param.9) | copy-start | bytes 368644
  12.7 12.4 %copy-start.2 = (bf16[512,4,128]{2,1,0:T(4,128)(2,1)S(1)}, bf16[512,4,128]{2,1,0:T(4,128)(2,1)}, u32[]{:S(2)}) copy-start(bf16[512,4,128]{2,1,0:T(4,128)(2,1)} %param.6) | copy-start | bytes 1572868
  12.7 12.6 %copy-start.6 = (bf16[512,4,128]{2,1,0:T(4,128)(2,1)S(1)}, bf16[512,4,128]{2,1,0:T(4,128)(2,1)}, u32[]{:S(2)}) copy-start(bf16[512,4,128]{2,1,0:T(4,128)(2,1)} %param.7) | copy-start | bytes 1572868
  12.7 105.3 %all-to-all-start = ((bf16[32,4,128,128]{3,2,1,0:T(8,128)(2,1)}), bf16[32,4,128,128]{3,2,1,0:T(8,128)(2,1)}, u32[]{:S(2)}, u32[]{:S(2)}) async-start(bf16[32,4,128,128]{3,2,1,0:T(8,128)(2,1)} %concatenate.6), calls=%async_computation | async-start | bytes 8388608 | tf_op jit(solution)/shard_map/all_to_all | solution.py:12
  48.6 7.0 %copy-start.19 = (f32[4,512,128]{2,1,0:T(8,128)S(1)}, f32[4,512,128]{2,1,0:T(8,128)}, u32[]{:S(2)}) copy-start(f32[4,512,128]{2,1,0:T(8,128)} %copy.120) | copy-start | bytes 3145732
  48.6 14.0 %copy-start.11 = (f32[512,4,512]{2,1,0:T(4,128)S(1)}, f32[512,4,512]{2,1,0:T(4,128)}, u32[]{:S(2)}) copy-start(f32[512,4,512]{2,1,0:T(4,128)} %fusion.12) | copy-start | bytes 12582916
  55.6 10.5 %copy-start.3 = (bf16[512,512]{0,1:T(8,128)(2,1)}, bf16[512,512]{0,1:T(8,128)(2,1)S(1)}, u32[]{:S(2)}) copy-start(bf16[512,512]{0,1:T(8,128)(2,1)S(1)} %get-tuple-element.37) | copy-start | bytes 1572868
  55.6 7.0 %copy-start.1 = (f32[4,512,512]{2,1,0:T(8,128)S(1)}, f32[4,512,512]{2,1,0:T(8,128)}, u32[]{:S(2)}) copy-start(f32[4,512,512]{2,1,0:T(8,128)} %fusion.66) | copy-start | bytes 12582916
  61.4 24.9 %collective-permute-start = (bf16[5,4,128,128]{2,3,0,1:T(8,128)(2,1)}, bf16[5,4,128,128]{2,3,0,1:T(8,128)(2,1)}, u32[]{:S(2)}, u32[]{:S(2)}) collective-permute-start(bf16[5,4,128,128]{2,3,0,1:T(8,128)(2,1)} %get-tuple-element.39), channel_id=1, source_target_pairs={{0,8},{8,0},{16,24},{24,16},{32,40},{40,32},{48,56},{56,48},{64,72... | collective-permute-start | bytes 1966088 | tf_op jit(solution)/shard_map/ppermute | solution.py:25
  82.0 1.9 copy-start.5
  82.0 5.6 %copy-start.20 = (f32[5,4,128,128]{2,3,0,1:T(8,128)S(1)}, f32[5,4,128,128]{2,3,0,1:T(8,128)}, u32[]{:S(2)}) copy-start(f32[5,4,128,128]{2,3,0,1:T(8,128)} %get-tuple-element.40) | copy-start | bytes 3932164
  88.9 61.6 %collective-permute-start.1 = (bf16[4,4,128,128]{2,3,0,1:T(8,128)(2,1)}, bf16[4,4,128,128]{2,3,0,1:T(8,128)(2,1)}, u32[]{:S(2)}, u32[]{:S(2)}) collective-permute-start(bf16[4,4,128,128]{2,3,0,1:T(8,128)(2,1)} %get-tuple-element.28), channel_id=1, source_target_pairs={{0,16},{16,0},{8,24},{24,8},{32,48},{48,32},{40,56},{56,40},{64,80... | collective-permute-start | bytes 1572872 | tf_op jit(solution)/shard_map/ppermute | solution.py:25
  122.8 2.0 copy-start.8
  122.8 2.0 copy-start.18
  123.1 0.8 copy-start.10
  141.7 6.8 %copy-start.4 = (bf16[512,512]{0,1:T(8,128)(2,1)S(1)}, bf16[512,512]{0,1:T(8,128)(2,1)}, u32[]{:S(2)}) copy-start(bf16[512,512]{0,1:T(8,128)(2,1)} %copy-done.3) | copy-start | bytes 1572868
  141.7 55.6 %all-to-all-start.1 = ((bf16[8,512,512]{1,2,0:T(8,128)(2,1)}), bf16[8,512,512]{1,2,0:T(8,128)(2,1)}, u32[]{:S(2)}, u32[]{:S(2)}) async-start(bf16[8,512,512]{1,2,0:T(8,128)(2,1)} %bitcast.98), calls=%async_computation.1 | async-start | bytes 8388608 | tf_op jit(solution)/shard_map/all_to_all | solution.py:35
  148.4 4.2 %copy-start.15 = (f32[4,4,128,128]{2,3,0,1:T(8,128)S(1)}, f32[4,4,128,128]{2,3,0,1:T(8,128)}, u32[]{:S(2)}) copy-start(f32[4,4,128,128]{2,3,0,1:T(8,128)} %get-tuple-element.29) | copy-start | bytes 3145732
  148.4 7.2 %copy-start.9 = (bf16[5,4,128,128]{3,2,1,0:T(8,128)(2,1)S(1)}, bf16[5,4,128,128]{3,2,1,0:T(8,128)(2,1)}, u32[]{:S(2)}) copy-start(bf16[5,4,128,128]{3,2,1,0:T(8,128)(2,1)} %copy-done.8) | copy-start | bytes 1966084
  151.6 1.0 copy-start.14
  153.8 11.5 %collective-permute-start.2 = (bf16[3,4,128,128]{2,3,0,1:T(8,128)(2,1)}, bf16[3,4,128,128]{2,3,0,1:T(8,128)(2,1)}, u32[]{:S(2)}, u32[]{:S(2)}) collective-permute-start(bf16[3,4,128,128]{2,3,0,1:T(8,128)(2,1)} %get-tuple-element.26), channel_id=1, source_target_pairs={{0,32},{32,0},{8,40},{40,8},{16,48},{48,16},{24,56},{56,24},{64,96... | collective-permute-start | bytes 1179656 | tf_op jit(solution)/shard_map/ppermute | solution.py:25
  160.1 6.2 %copy-start.16 = (f32[3,4,128,128]{2,3,0,1:T(8,128)S(1)}, f32[3,4,128,128]{2,3,0,1:T(8,128)}, u32[]{:S(2)}) copy-start(f32[3,4,128,128]{2,3,0,1:T(8,128)} %get-tuple-element.27) | copy-start | bytes 2359300
  160.1 7.9 %copy-start.17 = (f32[5,4,128,128]{2,3,0,1:T(8,128)S(1)}, f32[5,4,128,128]{2,3,0,1:T(8,128)}, u32[]{:S(2)}) copy-start(f32[5,4,128,128]{2,3,0,1:T(8,128)} %fusion.86) | copy-start | bytes 3932164
  166.4 24.8 %copy-start.13 = (f32[512,4,128]{2,0,1:T(8,128)S(1)}, f32[512,4,128]{2,0,1:T(8,128)}, u32[]{:S(2)}) copy-start(f32[512,4,128]{2,0,1:T(8,128)} %convolution_bitcast_fusion) | copy-start | bytes 3145732
  166.4 14.0 %collective-permute-start.3 = (bf16[2,4,128,128]{2,3,0,1:T(8,128)(2,1)S(1)}, bf16[2,4,128,128]{2,3,0,1:T(8,128)(2,1)S(1)}, u32[]{:S(2)}, u32[]{:S(2)}) collective-permute-start(bf16[2,4,128,128]{2,3,0,1:T(8,128)(2,1)S(1)} %get-tuple-element.24), channel_id=1, source_target_pairs={{0,64},{64,0},{8,72},{72,8},{16,80},{80,16},{24,88},{88,24},{32,96... | collective-permute-start | bytes 786440 | tf_op jit(solution)/shard_map/ppermute | solution.py:25
  180.6 10.2 %collective-permute-start.4 = (bf16[1,4,128,128]{2,3,0,1:T(8,128)(2,1)S(1)}, bf16[1,4,128,128]{2,3,0,1:T(8,128)(2,1)S(1)}, u32[]{:S(2)}, u32[]{:S(2)}) collective-permute-start(bf16[1,4,128,128]{2,3,0,1:T(8,128)(2,1)S(1)} %get-tuple-element.32), channel_id=1, source_target_pairs={{0,128},{128,0},{8,136},{136,8},{16,144},{144,16},{24,152},{152,24... | collective-permute-start | bytes 393224 | tf_op jit(solution)/shard_map/ppermute | solution.py:25
  183.4 9.4 %copy-start.7 = (bf16[512,4,128]{2,1,0:T(4,128)(2,1)S(1)}, bf16[512,4,128]{2,1,0:T(4,128)(2,1)}, u32[]{:S(2)}) copy-start(bf16[512,4,128]{2,1,0:T(4,128)(2,1)} %param.7) | copy-start | bytes 1572868
  191.0 2.1 %copy-start.12 = (f32[4,128,512]{2,1,0:T(8,128)S(1)}, f32[4,128,512]{2,1,0:T(8,128)}, u32[]{:S(2)}) copy-start(f32[4,128,512]{2,1,0:T(8,128)} %fusion.120) | copy-start | bytes 3145732
Sparse Core Ops, SparseCore 0:
  9.8 38.7 all-gather.1
